TPU v7x, 256 devices: a whole 4x4x8 slice. The times are simulated.
256 devices in a mesh: req: 32 (over z, y), tp: 8 (over x, core).
Axes of the slice: x: 4, y: 4, z: 8, core: 2. Of those that a mesh axis runs over, the one named last changes fastest.
Arguments:
- hidden: bfloat16 [9472, 5120], P('req', 'tp'), may hold values from -6 to 6
- raw_q: bfloat16 [9472, 3072], P('req', 'tp'), may hold values from -70 to 70
- raw_k: bfloat16 [9472, 3072], P('req', 'tp'), may hold values from -70 to 70
- raw_v: bfloat16 [9472, 3072], P('req', 'tp'), may hold values from -6 to 6
- q_gain: float32 [3072], P('tp'), may hold values from 0.5 to 2
- k_gain: float32 [3072], P('tp'), may hold values from 0.5 to 2
- out_weight: bfloat16 [3072, 5120], P('tp'), may hold values from -0.109375 to 0.109375
- post_gain: float32 [5120], P('tp'), may hold values from 0.25 to 1.75
- prefix_keys: bfloat16 [32, 32, 128, 3072], P(None, 'req', None, 'tp'), may hold values from -420 to 420
- prefix_values: bfloat16 [32, 32, 128, 3072], P(None, 'req', None, 'tp'), may hold values from -6 to 6
- key_cache: bfloat16 [256, 128, 3072], P('req', None, 'tp'), may hold values from -420 to 420
- value_cache: bfloat16 [256, 128, 3072], P('req', None, 'tp'), may hold values from -6 to 6
- slot_owner: int32 [256], P('req'), may hold values from -1 to 255, as said below
- slot_page: int32 [256], P('req'), may hold values from 0 to 127, as said below
- cache_lengths: int32 [256], replicated, may hold values from 0 to 16384, as said below
- span_offsets: int32 [32], replicated, may hold values from 0 to 4096
Outputs:
- new_hidden: bfloat16 [9472, 5120], P('req', 'tp')
Inputs may be any that keep to these rules, and one draw needn't show every extreme that they name: Each pool slot holds one page of decode request slot_owner[s], or nothing where it is -1. No page of a request is held twice, and a request holding c pages holds pages 0 to c - 1. `slot_page`: 0 for a slot that holds nothing. `cache_lengths`: A request holding c pages of the pool has a length from (c - 1) * 128 + 1 to c * 128, and 0 where c = 0.
All inputs are finite; a program needn't handle non-finite values.
Results may differ from a plain program's by a relative error of at most 0.0076.
Values may be sent and summed in bfloat16 or wider, within the bound.
A program may use at most 128 MiB of HBM per device.

v0:
```python
import jax
import jax.numpy as jnp
from jax import lax
from jax.sharding import PartitionSpec as P

HD = 128
SPAN = 288
DEC = 8
EPSILON = 1e-06
THETA = 500000.0
NEGATIVE = -1e30


def rotate(values, positions):
    half_width = values.shape[-1] // 2
    frequency = THETA ** (-(jnp.arange(half_width, dtype=jnp.float32) * 2.0 / values.shape[-1]))
    angles = positions.astype(jnp.float32)[:, None] * frequency[None, :]
    cosine = jnp.cos(angles)[:, None, :]
    sine_part = jnp.sin(angles)[:, None, :]
    first_half = values[..., :half_width]
    second = values[..., half_width:]
    return jnp.concatenate(
        [first_half * cosine - second * sine_part, second * cosine + first_half * sine_part], -1
    )


def softmax_part(scores, key_mask, values, form):
    masked = jnp.where(key_mask, scores, NEGATIVE)
    top_score = jnp.max(masked, -1)
    exp_terms = jnp.where(key_mask, jnp.exp(masked - top_score[..., None]), 0.0)
    weight_sum = jnp.sum(exp_terms, -1)
    numerator = jnp.einsum(
        form, exp_terms.astype(jnp.bfloat16), values, preferred_element_type=jnp.float32
    )
    return (top_score, weight_sum, numerator)


def merge_parts(top_scores, weight_sums, numerators):
    best_score = jnp.max(top_scores, 0)
    factor = jnp.exp(top_scores - best_score[None])
    weight_sum = jnp.sum(factor * weight_sums, 0)
    numerator = jnp.sum(factor[..., None] * numerators, 0)
    return numerator / weight_sum[..., None]


def body(
    hidden,
    raw_q,
    raw_k,
    raw_v,
    q_gain,
    k_gain,
    out_weight,
    post_gain,
    prefix_keys,
    prefix_values,
    key_cache,
    value_cache,
    slot_owner,
    slot_page,
    cache_lengths,
    span_offsets,
):
    groups = lax.axis_size("req")
    my_group = lax.axis_index("req")
    tp_count = lax.axis_size("tp")
    tp_index = lax.axis_index("tp")
    rows_group = SPAN + DEC
    local_width = raw_q.shape[1]
    local_heads = local_width // HD
    requests = groups * DEC
    score_scale = HD ** (-0.5)
    page_rows = key_cache.shape[1]
    own_lengths = lax.dynamic_slice_in_dim(cache_lengths, my_group * DEC, DEC)
    positions = jnp.concatenate(
        [span_offsets[my_group] + jnp.arange(SPAN, dtype=jnp.int32), own_lengths]
    )
    float_query = raw_q.astype(jnp.float32)
    float_key = raw_k.astype(jnp.float32)
    query_power, key_power = lax.psum(
        (jnp.sum(float_query * float_query, 1), jnp.sum(float_key * float_key, 1)), "tp"
    )
    full_width = local_width * tp_count
    normed_query = (
        float_query * lax.rsqrt(query_power / full_width + EPSILON)[:, None] * q_gain[None, :]
    )
    normed_key = float_key * lax.rsqrt(key_power / full_width + EPSILON)[:, None] * k_gain[None, :]
    query = rotate(normed_query.reshape(rows_group, local_heads, HD), positions).astype(
        jnp.bfloat16
    )
    key_rows = rotate(normed_key.reshape(rows_group, local_heads, HD), positions).astype(
        jnp.bfloat16
    )
    value_rows = raw_v.reshape(rows_group, local_heads, HD)
    causal = jnp.arange(SPAN)[:, None] >= jnp.arange(SPAN)[None, :]
    self_scores = (
        jnp.einsum(
            "qhd,khd->qhk", query[:SPAN], key_rows[:SPAN], preferred_element_type=jnp.float32
        )
        * score_scale
    )
    self_top, self_total, self_numerator = softmax_part(
        self_scores, causal[:, None, :], value_rows[:SPAN], "qhk,khd->qhd"
    )
    own_scores = (
        jnp.sum(query[SPAN:].astype(jnp.float32) * key_rows[SPAN:].astype(jnp.float32), -1)
        * score_scale
    )
    own_total = jnp.ones_like(own_scores)
    own_numerator = value_rows[SPAN:].astype(jnp.float32)
    everyone = lax.all_gather(query, "req", axis=0, tiled=True)
    everyone = everyone.reshape(groups, rows_group, local_heads, HD)
    pages_here = prefix_keys.shape[1]
    block_keys = prefix_keys.reshape(groups, pages_here * page_rows, local_heads, HD)
    block_values = prefix_values.reshape(groups, pages_here * page_rows, local_heads, HD)
    key_pos = my_group * pages_here * page_rows + jnp.arange(
        pages_here * page_rows, dtype=jnp.int32
    )
    key_mask = key_pos[None, :] < span_offsets[:, None]
    scores = (
        jnp.einsum(
            "gqhd,gkhd->gqhk", everyone[:, :SPAN], block_keys, preferred_element_type=jnp.float32
        )
        * score_scale
    )
    pre_top, pre_total, pre_numerator = softmax_part(
        scores, key_mask[:, None, None, :], block_values, "gqhk,gkhd->gqhd"
    )
    live_slot = slot_owner >= 0
    owner_index = jnp.maximum(slot_owner, 0)
    slot_queries = everyone[:, SPAN:].reshape(requests, local_heads, HD)[owner_index]
    slot_keys = key_cache.reshape(key_cache.shape[0], page_rows, local_heads, HD)
    slot_values = value_cache.reshape(value_cache.shape[0], page_rows, local_heads, HD)
    scores = (
        jnp.einsum("shd,sphd->shp", slot_queries, slot_keys, preferred_element_type=jnp.float32)
        * score_scale
    )
    key_pos = slot_page[:, None] * page_rows + jnp.arange(page_rows, dtype=jnp.int32)[None, :]
    key_mask = live_slot[:, None] & (key_pos < cache_lengths[owner_index][:, None])
    top_score, weight_sum, numerator = softmax_part(
        scores, key_mask[:, None, :], slot_values, "shp,sphd->shd"
    )
    member = slot_owner[None, :] == jnp.arange(requests, dtype=jnp.int32)[:, None]
    best_score = jnp.max(jnp.where(member[:, :, None], top_score[None], NEGATIVE), 1)
    factor = jnp.where(member[:, :, None], jnp.exp(top_score[None] - best_score[:, None]), 0.0)
    request_total = jnp.einsum("rsh,sh->rh", factor, weight_sum, precision=lax.Precision.HIGHEST)
    request_numerator = jnp.einsum(
        "rsh,shd->rhd", factor, numerator, precision=lax.Precision.HIGHEST
    )
    send_top = jnp.concatenate([pre_top, best_score.reshape(groups, DEC, local_heads)], 1).reshape(
        groups * rows_group, local_heads
    )
    send_total = jnp.concatenate(
        [pre_total, request_total.reshape(groups, DEC, local_heads)], 1
    ).reshape(groups * rows_group, local_heads)
    send_numerator = jnp.concatenate(
        [pre_numerator, request_numerator.reshape(groups, DEC, local_heads, HD)], 1
    ).reshape(groups * rows_group, local_heads, HD)
    back_top, back_total, back_numerator = (
        lax.all_to_all(send_top, "req", split_axis=0, concat_axis=0, tiled=True),
        lax.all_to_all(send_total, "req", split_axis=0, concat_axis=0, tiled=True),
        lax.all_to_all(send_numerator, "req", split_axis=0, concat_axis=0, tiled=True),
    )
    local_top = jnp.concatenate([self_top, own_scores], 0)
    local_total = jnp.concatenate([self_total, own_total], 0)
    local_numerator = jnp.concatenate([self_numerator, own_numerator], 0)
    merged = merge_parts(
        jnp.concatenate([back_top.reshape(groups, rows_group, local_heads), local_top[None]], 0),
        jnp.concatenate(
            [back_total.reshape(groups, rows_group, local_heads), local_total[None]], 0
        ),
        jnp.concatenate(
            [back_numerator.reshape(groups, rows_group, local_heads, HD), local_numerator[None]], 0
        ),
    )
    attention = merged.reshape(rows_group, local_width).astype(jnp.bfloat16)
    share_width = post_gain.shape[0]
    projected = lax.psum(jnp.dot(attention, out_weight, preferred_element_type=jnp.float32), "tp")
    inverse = lax.rsqrt(jnp.mean(projected * projected, 1) + EPSILON)
    my_share = lax.dynamic_slice_in_dim(projected, tp_index * share_width, share_width, 1)
    normed = my_share * inverse[:, None]
    return (hidden.astype(jnp.float32) + normed * post_gain[None, :]).astype(jnp.bfloat16)


def solution(mesh):
    return jax.shard_map(
        body,
        mesh=mesh,
        in_specs=(
            P("req", "tp"),
            P("req", "tp"),
            P("req", "tp"),
            P("req", "tp"),
            P("tp"),
            P("tp"),
            P("tp", None),
            P("tp"),
            P(None, "req", None, "tp"),
            P(None, "req", None, "tp"),
            P("req", None, "tp"),
            P("req", None, "tp"),
            P("req"),
            P("req"),
            P(),
            P(),
        ),
        out_specs=P("req", "tp"),
        check_vma=False,
    )
```

profile of v0, /device:TPU:1, one launch (start us, length us, event | category | flops | bytes accessed | tf_op | source)
XLA Modules:
  0.0 842.2 jit_solution(3925593860115718974)
XLA Ops:
  6.6 1.2 dynamic_slice.9
  9.5 1.1 fusion.24
  10.6 15.0 %all-reduce.1 = (f32[296]{0:T(512)S(1)}, f32[296]{0:T(512)S(1)}) all-reduce(f32[296]{0:T(512)S(1)} %fusion.24, f32[296]{0:T(512)S(1)} %fusion.22), channel_id=1, replica_groups=mesh['req'=32,'tp'=8] {'tp'}, use_global_device_ids=true, to_apply=%region_6.7 | all-reduce | flops 592 | bytes 4736 | tf_op jit(solution)/shard_map/psum | solution.py:80
  28.1 1.4 fusion.74
  29.5 1.5 fusion.75
  31.7 2.8 subtract_convert_fusion.1
  36.8 2.3 copy.97
  39.2 2.3 copy.104
  41.5 2.9 copy.94
  44.4 3.5 copy.102
  48.1 81.2 %all-gather.2.cloned.1.call-done = bf16[9472,3,128]{2,0,1:T(8,128)(2,1)} async-done(((bf16[296,3,128]{2,0,1:T(8,128)(2,1)}), bf16[9472,3,128]{2,0,1:T(8,128)(2,1)}) %all-gather.2.cloned.1.call-update) | async-done | bytes 7274512 | tf_op jit(solution)/shard_map/all_gather | solution.py:111
  131.0 1.4 fusion.47
  133.6 1.6 fusion.45
  135.2 1.3 convolution_bitcast_fusion.2
  136.5 14.0 %bitcast_reduce_fusion = (f32[32,288,3]{1,2,0:T(4,128)S(1)}, f32[32,3,288,128]{3,2,1,0:T(8,128)}) fusion(pred[32,128]{1,0:T(8,128)(4,1)S(1)} %broadcast_compare_fusion, bf16[32,128,3,128]{1,3,2,0:T(8,128)(2,1)} %bitcast.96, bf16[32,296,3,128]{3,1,0,2:T(8,128)(2,1)} %bitcast.102), kind=kOutput, calls=%fused_computation.6 | convolution fusion | flops 916558848 | bytes 24494080 | tf_op jit(solution)/shard_map/gqhd,gkhd->gqhk/dot_general | solution.py:121
  151.3 5.8 all-to-all-start
  157.1 11.8 %fusion.3 = f32[32,288,3]{1,2,0:T(4,128)} fusion(f32[32,3,288,128]{3,2,1,0:T(8,128)} %get-tuple-element.28, f32[32,288,3]{1,2,0:T(4,128)S(1)} %get-tuple-element.27, pred[32,128]{1,0:T(8,128)(4,1)S(1)} %broadcast_compare_fusion), kind=kLoop, calls=%fused_computation.10 | loop fusion | flops 17667072 | bytes 14381056 | tf_op jit(solution)/shard_map/reduce_sum | solution.py:31
  168.9 10.0 %convolution_bitcast_fusion = f32[32,288,3,128]{3,1,2,0:T(8,128)} fusion(bf16[32,128,3,128]{1,3,2,0:T(8,128)(2,1)S(1)} %bitcast.95, f32[32,3,288,128]{3,2,1,0:T(8,128)S(1)} %copy-done.1, f32[32,288,3]{1,2,0:T(4,128)S(1)} %get-tuple-element.27, pred[32,128]{1,0:T(8,128)(4,1)S(1)} %broadcast_compare_fusion), kind=kOutput, calls=%fused_computation.12 | convolution fusion | flops 923664384 | bytes 31571968 | tf_op jit(solution)/shard_map/gqhk,gkhd->gqhd/dot_general | solution.py:32
  179.2 1.2 copy.105
  180.4 1.7 pad_maximum_fusion.2
  182.1 9.0 %all-to-all-start.2 = ((f32[32,296,3]{1,2,0:T(4,128)}), f32[32,296,3]{1,2,0:T(4,128)S(1)}, u32[]{:S(2)}, u32[]{:S(2)}) async-start(f32[32,296,3]{1,2,0:T(4,128)} %pad_maximum_fusion.2), calls=%async_computation.2 | async-start | bytes 393216 | tf_op jit(solution)/shard_map/all_to_all | solution.py:161
  191.2 11.1 %pad_maximum_fusion = f32[32,296,3,128]{3,1,2,0:T(8,128)} fusion(f32[32,288,3,128]{3,1,2,0:T(8,128)} %convolution_bitcast_fusion, f32[256,3,128]{2,0,1:T(8,128)S(1)} %copy.105), kind=kLoop, calls=%fused_computation.4 | loop fusion | flops 3637248 | bytes 29097984 | tf_op jit(solution)/shard_map/concatenate | solution.py:156
  202.3 11.1 %copy.107 = f32[32,296,3,128]{3,1,0,2:T(8,128)} copy(f32[32,296,3,128]{3,1,2,0:T(8,128)} %pad_maximum_fusion) | data formatting | bytes 29097984 | tf_op jit(solution)/shard_map/concatenate | solution.py:156
  213.4 35.5 %copy.108 = f32[9472,3,128]{2,1,0:T(4,128)} copy(f32[9472,3,128]{2,0,1:T(8,128)} %bitcast.94) | data formatting | bytes 29097984 | tf_op jit(solution)/shard_map/reshape | solution.py:158
  249.0 9.5 %all-to-all-start.1 = ((f32[9472,3,128]{2,1,0:T(4,128)}), f32[9472,3,128]{2,1,0:T(4,128)}, u32[]{:S(2)}, u32[]{:S(2)}) async-start(f32[9472,3,128]{2,1,0:T(4,128)} %copy.108), calls=%async_computation.1 | async-start | bytes 38797312 | tf_op jit(solution)/shard_map/all_to_all | solution.py:162
  260.6 449.8 %all-to-all-done.1 = f32[9472,3,128]{2,1,0:T(4,128)} async-done(((f32[9472,3,128]{2,1,0:T(4,128)}), f32[9472,3,128]{2,1,0:T(4,128)}, u32[]{:S(2)}, u32[]{:S(2)}) %all-to-all-start.1) | async-done | bytes 14549024 | tf_op jit(solution)/shard_map/all_to_all | solution.py:162
  710.5 8.4 copy.111
  718.8 4.9 fusion
  723.8 4.4 fusion.26
  728.3 101.8 %all-reduce.4.cloned.1.call-done = f32[296,5120]{1,0:T(8,128)} async-done(((f32[296,5120]{1,0:T(8,128)}), f32[296,5120]{1,0:T(8,128)}) %all-reduce.4.cloned.1.call-update) | async-done | bytes 6062096 | tf_op jit(solution)/shard_map/psum | solution.py:178
  830.1 3.2 multiply_reduce_fusion
  833.3 2.1 add_convert_fusion
  (88 shorter events, 13.5 us)
Async XLA Ops:
  6.5 24.5 %copy-start = (s32[256]{0:T(256)S(1)}, s32[256]{0:T(256)}, u32[]{:S(2)}) copy-start(s32[256]{0:T(256)} %param.30) | copy-start | bytes 3076
  6.5 29.6 %copy-start.13 = (s32[8]{0:T(128)S(1)}, s32[8]{0:T(128)}, u32[]{:S(2)}) copy-start(s32[8]{0:T(128)} %param.28) | copy-start | bytes 100
  6.5 122.8 %all-gather.2.cloned.1.call-start = ((), (), s32[]{:S(2)}) async-start(), calls=%async_computation.3 | async-start | bytes 7501824 | tf_op jit(solution)/shard_map/all_gather | solution.py:111
  31.0 10.5 %copy-start.3 = (bf16[32,1,128,384]{3,2,1,0:T(8,128)(2,1)S(1)}, bf16[32,1,128,384]{3,2,1,0:T(8,128)(2,1)}, u32[]{:S(2)}) copy-start(bf16[32,1,128,384]{3,2,1,0:T(8,128)(2,1)} %param.24) | copy-start | bytes 9437188
  34.6 0.7 copy-start.4
  34.6 0.8 copy-start.6
  39.2 8.7 %copy-start.16 = (s32[8]{0:T(128)S(1)}, s32[8]{0:T(128)}, u32[]{:S(2)}) copy-start(s32[8]{0:T(128)} %param.29) | copy-start | bytes 100
  39.2 8.9 %copy-start.14 = (s32[32]{0:T(128)S(1)}, s32[32]{0:T(128)}, u32[]{:S(2)}) copy-start(s32[32]{0:T(128)} %param.31) | copy-start | bytes 388
  151.3 30.8 %all-to-all-start = ((f32[32,296,3]{1,2,0:T(4,128)}), f32[32,296,3]{1,2,0:T(4,128)S(1)}, u32[]{:S(2)}, u32[]{:S(2)}) async-start(f32[32,296,3]{1,2,0:T(4,128)} %pad_maximum_fusion.1), calls=%async_computation | async-start | bytes 393216 | tf_op jit(solution)/shard_map/all_to_all | solution.py:160
  157.0 11.8 %copy-start.1 = (f32[32,3,288,128]{3,2,1,0:T(8,128)S(1)}, f32[32,3,288,128]{3,2,1,0:T(8,128)}, u32[]{:S(2)}) copy-start(f32[32,3,288,128]{3,2,1,0:T(8,128)} %get-tuple-element.28) | copy-start | bytes 42467332
  168.9 10.0 %copy-start.12 = (f32[8,3]{0,1:T(4,128)S(1)}, f32[8,3]{0,1:T(4,128)}, u32[]{:S(2)}) copy-start(f32[8,3]{0,1:T(4,128)} %get-tuple-element.19) | copy-start | bytes 292
  182.1 66.9 %all-to-all-start.2 = ((f32[32,296,3]{1,2,0:T(4,128)}), f32[32,296,3]{1,2,0:T(4,128)S(1)}, u32[]{:S(2)}, u32[]{:S(2)}) async-start(f32[32,296,3]{1,2,0:T(4,128)} %pad_maximum_fusion.2), calls=%async_computation.2 | async-start | bytes 393216 | tf_op jit(solution)/shard_map/all_to_all | solution.py:161
  248.9 9.8 %copy-start.5 = (bf16[296,3,64]{2,0,1:T(8,128)(2,1)S(1)}, bf16[296,3,64]{2,0,1:T(8,128)(2,1)}, u32[]{:S(2)}) copy-start(bf16[296,3,64]{2,0,1:T(8,128)(2,1)} %copy-done.4) | copy-start | bytes 340996
  248.9 9.8 %copy-start.7 = (bf16[296,3,64]{2,0,1:T(8,128)(2,1)S(1)}, bf16[296,3,64]{2,0,1:T(8,128)(2,1)}, u32[]{:S(2)}) copy-start(bf16[296,3,64]{2,0,1:T(8,128)(2,1)} %copy-done.6) | copy-start | bytes 340996
  248.9 9.8 %copy-start.8 = (bf16[296,3,64]{2,0,1:T(8,128)(2,1)S(1)}, bf16[296,3,64]{2,0,1:T(8,128)(2,1)}, u32[]{:S(2)}) copy-start(bf16[296,3,64]{2,0,1:T(8,128)(2,1)} %get-tuple-element.17) | copy-start | bytes 340996
  248.9 9.8 %copy-start.9 = (bf16[296,3,64]{2,0,1:T(8,128)(2,1)S(1)}, bf16[296,3,64]{2,0,1:T(8,128)(2,1)}, u32[]{:S(2)}) copy-start(bf16[296,3,64]{2,0,1:T(8,128)(2,1)} %get-tuple-element.18) | copy-start | bytes 340996
  248.9 10.8 %copy-start.15 = (bf16[296,384]{1,0:T(8,128)(2,1)S(1)}, bf16[296,384]{1,0:T(8,128)(2,1)}, u32[]{:S(2)}) copy-start(bf16[296,384]{1,0:T(8,128)(2,1)} %param.19) | copy-start | bytes 681988
  249.0 461.5 %all-to-all-start.1 = ((f32[9472,3,128]{2,1,0:T(4,128)}), f32[9472,3,128]{2,1,0:T(4,128)}, u32[]{:S(2)}, u32[]{:S(2)}) async-start(f32[9472,3,128]{2,1,0:T(4,128)} %copy.108), calls=%async_computation.1 | async-start | bytes 38797312 | tf_op jit(solution)/shard_map/all_to_all | solution.py:162
  258.4 571.6 %all-reduce.4.cloned.1.call-start = ((), (), s32[]{:S(2)}) async-start(), calls=%async_computation.4 | async-start | bytes 12124160 | tf_op jit(solution)/shard_map/psum | solution.py:178
  718.8 5.0 copy-start.2
  728.2 105.0 %copy-start.10 = (bf16[296,640]{1,0:T(8,128)(2,1)S(1)}, bf16[296,640]{1,0:T(8,128)(2,1)}, u32[]{:S(2)}) copy-start(bf16[296,640]{1,0:T(8,128)(2,1)} %param.16) | copy-start | bytes 1136644
  728.2 105.0 %copy-start.11 = (f32[640]{0:T(1024)S(1)}, f32[640]{0:T(1024)}, u32[]{:S(2)}) copy-start(f32[640]{0:T(1024)} %param.23) | copy-start | bytes 7684
Sparse Core Ops, SparseCore 0:
  36.3 93.0 all-gather.1
  728.4 101.6 all-reduce.3
where the time goes:
time: 843 us; the launch traced here: 842 us
  waiting for transfers between devices  633 us (75%)
  local copies, waits for them, and re-layouts  75.1 us (9%)
  other arithmetic  46.9 us (6%)
  matrix products  34 us (4%)
  starting transfers between devices  24.5 us (3%)
  blocking collectives  15 us (2%)
  between operations  13.8 us (2%)
    all_to_all x1, waiting for transfers between devices, body(): lax.all_to_all(send_numerator, 'req', split_axis=0, concat_axis=0, tiled=...  450 us
    psum x1, waiting for transfers between devices, body(): lax.psum(jnp.dot(attention, out_weight, preferred_element_type=jnp.float3...  102 us
    all_gather x1, waiting for transfers between devices, body(): everyone = lax.all_gather(query, 'req', axis=0, tiled=True)  81.2 us
    reshape x1, local copies, waits for them, and re-layouts, body(): send_numerator = jnp.concatenate([pre_numerator, request_numerator.reshap...  35.5 us
  transfers between devices with their start and end apart: 5, of which 3 were waited for; matrix products, arithmetic and copies ran while one was open for 11% of the time, Pallas kernels for 0%

commit v1 on v0

--- a/solution.py
+++ b/solution.py
@@ -175,7 +175,10 @@
     )
     attention = merged.reshape(rows_group, local_width).astype(jnp.bfloat16)
     share_width = post_gain.shape[0]
-    projected = lax.psum(jnp.dot(attention, out_weight, preferred_element_type=jnp.float32), "tp")
+    projected = jnp.sum(
+        lax.all_gather(jnp.dot(attention, out_weight, preferred_element_type=jnp.float32), "tp"),
+        axis=0,
+    )
     inverse = lax.rsqrt(jnp.mean(projected * projected, 1) + EPSILON)
     my_share = lax.dynamic_slice_in_dim(projected, tp_index * share_width, share_width, 1)
     normed = my_share * inverse[:, None]

time: 843 us -> 1010 us (1.20)
  waiting for transfers between devices: 633 us -> 768 us
  other arithmetic: 46.9 us -> 73.5 us
    all_gather x0 -> x1, waiting for transfers between devices: none -> 233 us  [body(): lax.all_gather(jnp.dot(attention, out_weight, preferred_element_type=jnp....]
    psum x1 -> x0, waiting for transfers between devices: 102 us -> none  [body(): lax.psum(jnp.dot(attention, out_weight, preferred_element_type=jnp.float3...]
    reduce_sum x0 -> x1, other arithmetic: none -> 26.4 us  [body(): jnp.sum(lax.all_gather(jnp.dot(attention, out_weight, preferred_element_t...]
  transfers between devices with their start and end apart: 5 -> 5, of which waited for: 3 -> 3; matrix products, arithmetic and copies ran while one was open for 11% -> 10% of each run, Pallas kernels for 0% -> 0%
where the time goes in v1:
time: 1010 us; the launch traced here: 1000 us
  waiting for transfers between devices  768 us (76%)
  local copies, waits for them, and re-layouts  75.1 us (7%)
  other arithmetic  73.5 us (7%)
  matrix products  34 us (3%)
  starting transfers between devices  24.5 us (2%)
  blocking collectives  15 us (1%)
  between operations  13.8 us (1%)
    all_to_all x1, waiting for transfers between devices, body(): lax.all_to_all(send_numerator, 'req', split_axis=0, concat_axis=0, tiled=...  454 us
    all_gather x1, waiting for transfers between devices, body(): lax.all_gather(jnp.dot(attention, out_weight, preferred_element_type=jnp....  233 us
    all_gather x1, waiting for transfers between devices, body(): everyone = lax.all_gather(query, 'req', axis=0, tiled=True)  81.2 us
    reshape x1, local copies, waits for them, and re-layouts, body(): send_numerator = jnp.concatenate([pre_numerator, request_numerator.reshap...  35.5 us
    reduce_sum x1, other arithmetic, body(): jnp.sum(lax.all_gather(jnp.dot(attention, out_weight, preferred_element_t...  26.4 us
  transfers between devices with their start and end apart: 5, of which 3 were waited for; matrix products, arithmetic and copies ran while one was open for 10% of the time, Pallas kernels for 0%

profile of v1, /device:TPU:1, one launch (start us, length us, event | category | flops | bytes accessed | tf_op | source)
XLA Modules:
  0.0 1004.1 jit_solution(1491034992551088360)
XLA Ops:
  6.6 1.2 dynamic_slice.9
  10.6 15.0 %all-reduce.1 = (f32[296]{0:T(512)S(1)}, f32[296]{0:T(512)S(1)}) all-reduce(f32[296]{0:T(512)S(1)} %fusion.24, f32[296]{0:T(512)S(1)} %fusion.22), channel_id=1, replica_groups=mesh['req'=32,'tp'=8] {'tp'}, use_global_device_ids=true, to_apply=%region_6.7 | all-reduce | flops 592 | bytes 4736 | tf_op jit(solution)/shard_map/psum | solution.py:80
  28.1 1.4 fusion.74
  29.5 1.5 fusion.75
  31.7 2.8 subtract_convert_fusion.1
  36.8 2.3 copy.97
  39.2 2.3 copy.104
  41.5 2.9 copy.94
  44.4 3.5 copy.102
  48.1 81.2 %all-gather.4.cloned.1.call-done = bf16[9472,3,128]{2,0,1:T(8,128)(2,1)} async-done(((bf16[296,3,128]{2,0,1:T(8,128)(2,1)}), bf16[9472,3,128]{2,0,1:T(8,128)(2,1)}) %all-gather.4.cloned.1.call-update) | async-done | bytes 7274512 | tf_op jit(solution)/shard_map/all_gather | solution.py:111
  131.0 1.4 fusion.47
  133.6 1.6 fusion.45
  135.2 1.3 convolution_bitcast_fusion.2
  136.5 14.0 %bitcast_reduce_fusion = (f32[32,288,3]{1,2,0:T(4,128)S(1)}, f32[32,3,288,128]{3,2,1,0:T(8,128)}) fusion(pred[32,128]{1,0:T(8,128)(4,1)S(1)} %broadcast_compare_fusion, bf16[32,128,3,128]{1,3,2,0:T(8,128)(2,1)} %bitcast.98, bf16[32,296,3,128]{3,1,0,2:T(8,128)(2,1)} %bitcast.104), kind=kOutput, calls=%fused_computation.6 | convolution fusion | flops 916558848 | bytes 24494080 | tf_op jit(solution)/shard_map/gqhd,gkhd->gqhk/dot_general | solution.py:121
  151.3 5.8 all-to-all-start
  157.1 11.9 %fusion.3 = f32[32,288,3]{1,2,0:T(4,128)} fusion(f32[32,3,288,128]{3,2,1,0:T(8,128)} %get-tuple-element.28, f32[32,288,3]{1,2,0:T(4,128)S(1)} %get-tuple-element.27, pred[32,128]{1,0:T(8,128)(4,1)S(1)} %broadcast_compare_fusion), kind=kLoop, calls=%fused_computation.10 | loop fusion | flops 17667072 | bytes 14381056 | tf_op jit(solution)/shard_map/reduce_sum | solution.py:31
  169.0 10.0 convolution_bitcast_fusion
  179.4 1.2 copy.105
  180.5 1.7 pad_maximum_fusion.2
  182.2 9.0 all-to-all-start.2
  191.3 11.2 %pad_maximum_fusion = f32[32,296,3,128]{3,1,2,0:T(8,128)} fusion(f32[32,288,3,128]{3,1,2,0:T(8,128)} %convolution_bitcast_fusion, f32[256,3,128]{2,0,1:T(8,128)S(1)} %copy.105), kind=kLoop, calls=%fused_computation.4 | loop fusion | flops 3637248 | bytes 29097984 | tf_op jit(solution)/shard_map/concatenate | solution.py:156
  202.4 11.1 %copy.107 = f32[32,296,3,128]{3,1,0,2:T(8,128)} copy(f32[32,296,3,128]{3,1,2,0:T(8,128)} %pad_maximum_fusion) | data formatting | bytes 29097984 | tf_op jit(solution)/shard_map/concatenate | solution.py:156
  213.6 35.5 %copy.108 = f32[9472,3,128]{2,1,0:T(4,128)} copy(f32[9472,3,128]{2,0,1:T(8,128)} %bitcast.95) | data formatting | bytes 29097984 | tf_op jit(solution)/shard_map/reshape | solution.py:158
  249.1 9.5 all-to-all-start.1
  260.8 453.6 %all-to-all-done.1 = f32[9472,3,128]{2,1,0:T(4,128)} async-done(((f32[9472,3,128]{2,1,0:T(4,128)}), f32[9472,3,128]{2,1,0:T(4,128)}, u32[]{:S(2)}, u32[]{:S(2)}) %all-to-all-start.1) | async-done | bytes 14549024 | tf_op jit(solution)/shard_map/all_to_all | solution.py:162
  714.4 8.4 copy.111
  722.7 4.9 fusion
  727.7 4.4 fusion.26
  732.2 233.4 %all-gather.6.cloned.1.call-done = f32[2368,5120]{1,0:T(8,128)} async-done(((f32[296,5120]{1,0:T(8,128)}), f32[2368,5120]{1,0:T(8,128)}) %all-gather.6.cloned.1.call-update) | async-done | bytes 48496656 | tf_op jit(solution)/shard_map/all_gather | solution.py:179
  965.5 26.4 %reduce_sum.98 = f32[296,5120]{1,0:T(8,128)} reduce(f32[8,296,5120]{2,1,0:T(8,128)} %bitcast.96, f32[]{:T(128)} %constant.23.clone.1), dimensions={0}, to_apply=%region_15.16 | reduce | flops 10608640 | bytes 54558724 | tf_op jit(solution)/shard_map/reduce_sum | solution.py:178
  992.0 3.2 multiply_reduce_fusion
  995.2 2.1 add_convert_fusion
  (89 shorter events, 14.6 us)
Async XLA Ops:
  6.5 24.5 %copy-start = (s32[256]{0:T(256)S(1)}, s32[256]{0:T(256)}, u32[]{:S(2)}) copy-start(s32[256]{0:T(256)} %param.30) | copy-start | bytes 3076
  6.5 29.6 %copy-start.13 = (s32[8]{0:T(128)S(1)}, s32[8]{0:T(128)}, u32[]{:S(2)}) copy-start(s32[8]{0:T(128)} %param.28) | copy-start | bytes 100
  6.5 122.8 %all-gather.4.cloned.1.call-start = ((), (), s32[]{:S(2)}) async-start(), calls=%async_computation.3 | async-start | bytes 7501824 | tf_op jit(solution)/shard_map/all_gather | solution.py:111
  31.0 10.5 %copy-start.3 = (bf16[32,1,128,384]{3,2,1,0:T(8,128)(2,1)S(1)}, bf16[32,1,128,384]{3,2,1,0:T(8,128)(2,1)}, u32[]{:S(2)}) copy-start(bf16[32,1,128,384]{3,2,1,0:T(8,128)(2,1)} %param.24) | copy-start | bytes 9437188
  34.6 0.7 copy-start.4
  34.6 0.8 copy-start.6
  39.2 8.7 copy-start.16
  39.2 8.9 copy-start.14
  151.3 30.9 %all-to-all-start = ((f32[32,296,3]{1,2,0:T(4,128)}), f32[32,296,3]{1,2,0:T(4,128)S(1)}, u32[]{:S(2)}, u32[]{:S(2)}) async-start(f32[32,296,3]{1,2,0:T(4,128)} %pad_maximum_fusion.1), calls=%async_computation | async-start | bytes 393216 | tf_op jit(solution)/shard_map/all_to_all | solution.py:160
  157.0 11.9 %copy-start.1 = (f32[32,3,288,128]{3,2,1,0:T(8,128)S(1)}, f32[32,3,288,128]{3,2,1,0:T(8,128)}, u32[]{:S(2)}) copy-start(f32[32,3,288,128]{3,2,1,0:T(8,128)} %get-tuple-element.28) | copy-start | bytes 42467332
  169.0 10.0 copy-start.12
  182.2 66.9 %all-to-all-start.2 = ((f32[32,296,3]{1,2,0:T(4,128)}), f32[32,296,3]{1,2,0:T(4,128)S(1)}, u32[]{:S(2)}, u32[]{:S(2)}) async-start(f32[32,296,3]{1,2,0:T(4,128)} %pad_maximum_fusion.2), calls=%async_computation.2 | async-start | bytes 393216 | tf_op jit(solution)/shard_map/all_to_all | solution.py:161
  249.1 9.8 copy-start.5
  249.1 9.8 copy-start.7
  249.1 9.8 copy-start.8
  249.1 9.8 copy-start.9
  249.1 10.8 %copy-start.15 = (bf16[296,384]{1,0:T(8,128)(2,1)S(1)}, bf16[296,384]{1,0:T(8,128)(2,1)}, u32[]{:S(2)}) copy-start(bf16[296,384]{1,0:T(8,128)(2,1)} %param.19) | copy-start | bytes 681988
  249.1 465.3 %all-to-all-start.1 = ((f32[9472,3,128]{2,1,0:T(4,128)}), f32[9472,3,128]{2,1,0:T(4,128)}, u32[]{:S(2)}, u32[]{:S(2)}) async-start(f32[9472,3,128]{2,1,0:T(4,128)} %copy.108), calls=%async_computation.1 | async-start | bytes 38797312 | tf_op jit(solution)/shard_map/all_to_all | solution.py:162
  258.6 706.9 %all-gather.6.cloned.1.call-start = ((), (), s32[]{:S(2)}) async-start(), calls=%async_computation.4 | async-start | bytes 54558720 | tf_op jit(solution)/shard_map/all_gather | solution.py:179
  722.7 5.0 copy-start.2
  965.5 29.7 %copy-start.10 = (bf16[296,640]{1,0:T(8,128)(2,1)S(1)}, bf16[296,640]{1,0:T(8,128)(2,1)}, u32[]{:S(2)}) copy-start(bf16[296,640]{1,0:T(8,128)(2,1)} %param.16) | copy-start | bytes 1136644
  965.5 29.7 %copy-start.11 = (f32[640]{0:T(1024)S(1)}, f32[640]{0:T(1024)}, u32[]{:S(2)}) copy-start(f32[640]{0:T(1024)} %param.23) | copy-start | bytes 7684
Sparse Core Ops, SparseCore 0:
  36.3 93.0 all-gather.3
  732.3 233.1 all-gather.5
